TPU v7x, 512 devices: a whole 4x4x16 slice. The times are simulated.
512 devices in a mesh: dp: 16 (over z), expert: 32 (over y, x, core).
Axes of the slice: x: 4, y: 4, z: 16, core: 2. Of those that a mesh axis runs over, the one named last changes fastest.
Arguments:
- tokens: bfloat16 [4096, 4096], P('expert', 'dp'), may hold values from -6 to 6
- routing: int32 [4096, 8], P('expert'), may hold values from 0 to 31, all different within a row; in each aligned block of 128 rows (0 to 127, 128 to 255, ...) at most 40 rows name the same one
- gate_probs: float32 [4096, 8], P('expert'), may hold values from 0.05 to 0.3
- paired: int32 [32], P('expert'), may hold values from 0 to 1, as said below
- w_gate: bfloat16 [32, 4096, 768], P('expert', 'dp'), may hold values from -0.09375 to 0.09375
- w_up: bfloat16 [32, 4096, 768], P('expert', 'dp'), may hold values from -0.09375 to 0.09375
- w_down: bfloat16 [32, 768, 4096], P('expert', None, 'dp'), may hold values from -0.21875 to 0.21875
- cotangent: bfloat16 [4096, 4096], P('expert', 'dp'), may hold values from -6 to 6
Outputs:
- output: bfloat16 [4096, 4096], P('expert', 'dp')
- grad_tokens: bfloat16 [4096, 4096], P('expert', 'dp')
- grad_gate: float32 [32, 4096, 768], P('expert', 'dp')
- grad_up: float32 [32, 4096, 768], P('expert', 'dp')
- grad_down: float32 [32, 768, 4096], P('expert', None, 'dp')
Inputs may be any that keep to these rules, and one draw needn't show every extreme that they name: `routing`: each token names 8 different copies; among the tokens of one source (aligned blocks of 128 tokens) no copy is named more than 40 times, a bound that some block reaches. paired[c] equals paired[(c + 16) mod 32]; paired[0] and paired[31] are 1.
All inputs are finite; a program needn't handle non-finite values.
Results may differ from a plain program's by a relative error of at most 0.029.
Values may be sent and summed in bfloat16 or wider, within the bound.
A program may use at most 64 MiB of HBM per device.

v0:
```python
import jax
import jax.numpy as jnp
from jax import lax
from jax.sharding import PartitionSpec as P


def swapped(value, axis, stride):
    mask = 2**stride
    pairs = [(source, source ^ mask) for source in range(lax.axis_size(axis))]
    return lax.ppermute(value, axis, pairs)


def product(left, right):
    return jnp.dot(left, right, preferred_element_type=jnp.float32)


def inner_rows(left, right):
    return lax.dot_general(
        left, right, (((0,), (0,)), ((), ())), preferred_element_type=jnp.float32
    )


def outer_cols(left, right):
    return lax.dot_general(
        left, right, (((1,), (1,)), ((), ())), preferred_element_type=jnp.float32
    )


def rounded(value):
    return lax.optimization_barrier(value.astype(jnp.bfloat16)).astype(jnp.float32)


def per_device(tokens, routing, gate_probs, paired, w_gate, w_up, w_down, cotangent):
    n_expert = lax.axis_size("expert")
    n_data = lax.axis_size("dp")
    token_count, top_count = routing.shape
    slab = tokens.shape[1]
    hidden = w_gate.shape[2]
    capacity = max(2, 5 * token_count * top_count // (4 * n_expert))
    all_rows = n_expert * capacity
    own_rows = all_rows // n_data
    gate_slab = w_gate[0]
    up_slab = w_up[0]
    down_slab = w_down[0]
    flat_route = routing.reshape(token_count * top_count)
    onehot = (flat_route[:, None] == jnp.arange(n_expert, dtype=jnp.int32)[None, :]).astype(
        jnp.int32
    )
    earlier = jnp.cumsum(onehot, axis=0) - onehot
    target = flat_route * capacity + jnp.sum(earlier * onehot, axis=1)
    select = jnp.arange(all_rows, dtype=jnp.int32)[:, None] == target[None, :]
    select_grid = select.reshape(all_rows, token_count, top_count)
    token_select = jnp.any(select_grid, axis=2).astype(jnp.bfloat16)
    weight_select = jnp.sum(select_grid.astype(jnp.float32) * gate_probs[None, :, :], axis=2)
    weight_high = weight_select.astype(jnp.bfloat16)
    weight_low = (weight_select - weight_high.astype(jnp.float32)).astype(jnp.bfloat16)
    send_tokens = product(token_select, tokens).astype(jnp.bfloat16)
    scaled = (gate_probs[:, :, None] * cotangent.astype(jnp.float32)[:, None, :]).astype(
        jnp.bfloat16
    )
    send_grads = product(
        select.astype(jnp.bfloat16), scaled.reshape(token_count * top_count, slab)
    ).astype(jnp.bfloat16)
    arrived = (
        lax.all_to_all(
            send_tokens.reshape(n_expert, capacity, slab),
            "expert",
            split_axis=0,
            concat_axis=0,
            tiled=True,
        ),
        lax.all_to_all(
            send_grads.reshape(n_expert, capacity, slab),
            "expert",
            split_axis=0,
            concat_axis=0,
            tiled=True,
        ),
    )
    token_slab = arrived[0].reshape(all_rows, slab)
    grad_slab = arrived[1].reshape(all_rows, slab)
    block_rows = token_slab
    summed = lax.psum_scatter(
        rounded(
            jnp.concatenate([product(block_rows, gate_slab), product(block_rows, up_slab)], axis=1)
        ).astype(jnp.bfloat16),
        "dp",
        scatter_dimension=0,
        tiled=True,
    ).astype(jnp.float32)
    gate_own = summed[:, :hidden]
    up_own = summed[:, hidden:]
    hid_own = (jax.nn.silu(gate_own) * up_own).astype(jnp.bfloat16)
    piece = lax.all_gather(hid_own, "dp", axis=0, tiled=True)
    answer_acc = product(piece, down_slab)
    grad_down = inner_rows(piece, grad_slab)
    answer_slab = answer_acc.astype(jnp.bfloat16)
    answer_back = lax.all_to_all(
        answer_slab.reshape(n_expert, capacity, slab),
        "expert",
        split_axis=0,
        concat_axis=0,
        tiled=True,
    )
    hidden_parts = (
        outer_cols(grad_slab, down_slab).astype(jnp.bfloat16).reshape(n_data, own_rows, hidden)
    )
    arrived_parts = lax.all_to_all(hidden_parts, "dp", split_axis=0, concat_axis=0, tiled=True)
    grad_hidden = jnp.sum(arrived_parts.astype(jnp.float32), axis=0)
    sigma = jax.nn.sigmoid(gate_own)
    activated = gate_own * sigma
    grad_gate_rows = (grad_hidden * up_own * sigma * (1.0 + gate_own * (1.0 - sigma))).astype(
        jnp.bfloat16
    )
    grad_up_rows = (grad_hidden * activated).astype(jnp.bfloat16)
    piece_gate = lax.all_gather(grad_gate_rows, "dp", axis=0, tiled=True)
    piece_up = lax.all_gather(grad_up_rows, "dp", axis=0, tiled=True)
    block_rows = token_slab
    gate_acc = inner_rows(block_rows, piece_gate)
    up_acc = inner_rows(block_rows, piece_up)
    back_rows = outer_cols(piece_gate, gate_slab) + outer_cols(piece_up, up_slab)
    grad_gate = gate_acc
    grad_up = up_acc
    back_slab = back_rows.astype(jnp.bfloat16)
    back_rows_home = lax.all_to_all(
        back_slab.reshape(n_expert, capacity, slab),
        "expert",
        split_axis=0,
        concat_axis=0,
        tiled=True,
    )
    answer_home = answer_back.reshape(all_rows, slab)
    output = (inner_rows(weight_high, answer_home) + inner_rows(weight_low, answer_home)).astype(
        jnp.bfloat16
    )
    grad_tokens = inner_rows(token_select, back_rows_home.reshape(all_rows, slab)).astype(
        jnp.bfloat16
    )
    other = (
        swapped(grad_gate.astype(jnp.bfloat16), "expert", n_expert.bit_length() - 2).astype(
            grad_gate.dtype
        ),
        swapped(grad_up.astype(jnp.bfloat16), "expert", n_expert.bit_length() - 2).astype(
            grad_up.dtype
        ),
        swapped(grad_down.astype(jnp.bfloat16), "expert", n_expert.bit_length() - 2).astype(
            grad_down.dtype
        ),
    )
    keep = paired.astype(jnp.float32)[0]
    grad_gate = (grad_gate + keep * other[0])[None]
    grad_up = (grad_up + keep * other[1])[None]
    grad_down = (grad_down + keep * other[2])[None]
    return (output, grad_tokens, grad_gate, grad_up, grad_down)


def solution(mesh):
    return jax.shard_map(
        per_device,
        mesh=mesh,
        in_specs=(
            P("expert", "dp"),
            P("expert", None),
            P("expert", None),
            P("expert"),
            P("expert", "dp", None),
            P("expert", "dp", None),
            P("expert", None, "dp"),
            P("expert", "dp"),
        ),
        out_specs=(
            P("expert", "dp"),
            P("expert", "dp"),
            P("expert", "dp", None),
            P("expert", "dp", None),
            P("expert", None, "dp"),
        ),
        check_vma=False,
    )
```

profile of v0, /device:TPU:1, one launch (start us, length us, event | category | flops | bytes accessed | tf_op | source)
XLA Modules:
  0.0 480.7 jit_solution(16176602574999856850)
XLA Ops:
  8.2 9.0 %reduce-window.6 = s32[32,8,128]{2,1,0:T(8,128)S(1)} reduce-window(s32[32,8,128]{2,1,0:T(8,128)S(1)} %fusion.24, s32[]{:T(128)} %constant.7.clone.1), window={size=1x1x128 pad=0_0x0_0x127_0}, to_apply=%region_0.0 | reduce-window | flops 4161536 | bytes 262148 | tf_op jit(solution)/shard_map/reduce-window
  18.6 4.6 fusion
  23.3 2.1 convolution_convert_fusion.4
  25.3 10.4 %all-to-all-start = ((bf16[32,40,256]{2,1,0:T(8,128)(2,1)}), bf16[32,40,256]{2,1,0:T(8,128)(2,1)S(1)}, u32[]{:S(2)}, u32[]{:S(2)}) async-start(bf16[32,40,256]{2,1,0:T(8,128)(2,1)} %bitcast.2), calls=%async_computation | async-start | bytes 1310720 | tf_op jit(solution)/shard_map/all_to_all | solution.py:65
  36.0 1.9 fusion.4
  38.0 10.8 %all-to-all-done = bf16[32,40,256]{2,1,0:T(8,128)(2,1)S(1)} async-done(((bf16[32,40,256]{2,1,0:T(8,128)(2,1)}), bf16[32,40,256]{2,1,0:T(8,128)(2,1)S(1)}, u32[]{:S(2)}, u32[]{:S(2)}) %all-to-all-start) | async-done | bytes 655392 | tf_op jit(solution)/shard_map/all_to_all | solution.py:65
  48.8 4.2 all-to-all-start.2
  54.5 2.1 pad_maximum_fusion
  56.7 6.3 %copy.48 = bf16[1280,1536]{1,0:T(8,128)(2,1)} copy(bf16[1280,1536]{0,1:T(8,128)(2,1)} %pad_maximum_fusion) | data formatting | bytes 7864320
  63.0 3.0 all-to-all-done.2
  66.8 117.4 %all_to_all.25 = bf16[16,80,768]{2,1,0:T(8,128)(2,1)S(1)} all-to-all(bf16[16,80,768]{2,1,0:T(8,128)(2,1)S(1)} %bitcast.77), channel_id=1, replica_groups=mesh['dp'=16,'expert'=32] {'dp'}, dimensions={0} | all-to-all | bytes 3932160 | tf_op jit(solution)/shard_map/all_to_all | solution.py:108
  184.5 27.7 %reduce-scatter.4.cloned.1.call-done = bf16[80,1536]{1,0:T(8,128)(2,1)} async-done(((bf16[1280,1536]{1,0:T(8,128)(2,1)}), bf16[80,1536]{1,0:T(8,128)(2,1)}) %reduce-scatter.4.cloned.1.call-update) | async-done | bytes 245776 | tf_op jit(solution)/shard_map/reduce_scatter | solution.py:83
  212.2 1.0 convert_element_type.90
  216.1 6.8 %select_reduce_fusion = f32[1280,128]{1,0:T(8,128)S(1)} fusion(f32[128,8]{0,1:T(8,128)S(1)} %copy-done.12, s32[128,8]{0,1:T(8,128)S(1)} %multiply_add_fusion.1), kind=kLoop, calls=%fused_computation.1 | loop fusion | flops 3768320 | bytes 663552 | tf_op jit(solution)/shard_map/reduce_sum | solution.py:54
  222.8 56.5 %all-gather.4.cloned.1.call-done = bf16[1280,768]{1,0:T(8,128)(2,1)} async-done(((bf16[80,768]{1,0:T(8,128)(2,1)}), bf16[1280,768]{1,0:T(8,128)(2,1)}) %all-gather.4.cloned.1.call-update) | async-done | bytes 1966096 | tf_op jit(solution)/shard_map/all_gather | solution.py:94
  279.3 3.1 convolution_convert_fusion.3
  282.4 17.4 %all-to-all-start.1 = ((bf16[32,40,256]{2,1,0:T(8,128)(2,1)}), bf16[32,40,256]{2,1,0:T(8,128)(2,1)S(1)}, u32[]{:S(2)}, u32[]{:S(2)}) async-start(bf16[32,40,256]{2,1,0:T(8,128)(2,1)} %bitcast.7), calls=%async_computation.1 | async-start | bytes 1310720 | tf_op jit(solution)/shard_map/all_to_all | solution.py:98
  299.7 52.7 %all-gather.6.cloned.1.call-done = bf16[1280,768]{1,0:T(8,128)(2,1)} async-done(((bf16[80,768]{1,0:T(8,128)(2,1)}), bf16[1280,768]{1,0:T(8,128)(2,1)}) %all-gather.6.cloned.1.call-update) | async-done | bytes 1966096 | tf_op jit(solution)/shard_map/all_gather | solution.py:116
  352.4 3.0 fusion.25
  355.4 4.6 collective-permute-start
  360.1 64.6 %all-gather.8.cloned.1.call-done = bf16[1280,768]{1,0:T(8,128)(2,1)} async-done(((bf16[80,768]{1,0:T(8,128)(2,1)}), bf16[1280,768]{1,0:T(8,128)(2,1)}) %all-gather.8.cloned.1.call-update) | async-done | bytes 1966096 | tf_op jit(solution)/shard_map/all_gather | solution.py:117
  424.7 2.4 fusion.26
  427.1 4.8 collective-permute-start.1
  431.9 1.7 fusion.27
  433.6 2.3 collective-permute-start.2
  436.6 1.6 fusion.3
  438.2 2.0 add_bitcast_fusion.2
  440.2 1.0 add_bitcast_fusion.1
  441.1 18.0 %all-to-all-start.4 = ((bf16[32,40,256]{2,1,0:T(8,128)(2,1)}), bf16[32,40,256]{2,1,0:T(8,128)(2,1)}, u32[]{:S(2)}, u32[]{:S(2)}) async-start(bf16[32,40,256]{2,1,0:T(8,128)(2,1)} %bitcast.13), calls=%async_computation.4 | async-start | bytes 1310720 | tf_op jit(solution)/shard_map/all_to_all | solution.py:125
  459.1 2.0 add_bitcast_fusion
  462.3 9.8 %all-to-all-done.4 = bf16[32,40,256]{2,1,0:T(8,128)(2,1)} async-done(((bf16[32,40,256]{2,1,0:T(8,128)(2,1)}), bf16[32,40,256]{2,1,0:T(8,128)(2,1)}, u32[]{:S(2)}, u32[]{:S(2)}) %all-to-all-start.4) | async-done | bytes 655392 | tf_op jit(solution)/shard_map/all_to_all | solution.py:125
  472.1 2.1 convolution_convert_fusion.5
  (66 shorter events, 9.3 us)
Async XLA Ops:
  7.2 58.9 %copy-start = (bf16[1,768,256]{2,1,0:T(8,128)(2,1)S(1)}, bf16[1,768,256]{2,1,0:T(8,128)(2,1)}, u32[]{:S(2)}) copy-start(bf16[1,768,256]{2,1,0:T(8,128)(2,1)} %param.14) | copy-start | bytes 1179652
  8.0 27.8 %copy-start.11 = (bf16[128,256]{1,0:T(8,128)(2,1)S(1)}, bf16[128,256]{1,0:T(8,128)(2,1)}, u32[]{:S(2)}) copy-start(bf16[128,256]{1,0:T(8,128)(2,1)} %param.15) | copy-start | bytes 196612
  8.2 27.6 %copy-start.12 = (f32[128,8]{0,1:T(8,128)S(1)}, f32[128,8]{0,1:T(8,128)}, u32[]{:S(2)}) copy-start(f32[128,8]{0,1:T(8,128)} %param.10) | copy-start | bytes 12292
  23.3 2.1 copy-start.9
  25.3 23.5 %all-to-all-start = ((bf16[32,40,256]{2,1,0:T(8,128)(2,1)}), bf16[32,40,256]{2,1,0:T(8,128)(2,1)S(1)}, u32[]{:S(2)}, u32[]{:S(2)}) async-start(bf16[32,40,256]{2,1,0:T(8,128)(2,1)} %bitcast.2), calls=%async_computation | async-start | bytes 1310720 | tf_op jit(solution)/shard_map/all_to_all | solution.py:65
  36.0 17.1 %copy-start.6 = (bf16[1,256,768]{2,1,0:T(8,128)(2,1)S(1)}, bf16[1,256,768]{2,1,0:T(8,128)(2,1)}, u32[]{:S(2)}) copy-start(bf16[1,256,768]{2,1,0:T(8,128)(2,1)} %param.13) | copy-start | bytes 1179652
  48.8 5.0 %copy-start.5 = (bf16[1,256,768]{2,1,0:T(8,128)(2,1)S(1)}, bf16[1,256,768]{2,1,0:T(8,128)(2,1)}, u32[]{:S(2)}) copy-start(bf16[1,256,768]{2,1,0:T(8,128)(2,1)} %param.12) | copy-start | bytes 1179652
  48.8 17.3 %all-to-all-start.2 = ((bf16[32,40,256]{2,1,0:T(8,128)(2,1)}), bf16[32,40,256]{2,1,0:T(8,128)(2,1)S(1)}, u32[]{:S(2)}, u32[]{:S(2)}) async-start(bf16[32,40,256]{2,1,0:T(8,128)(2,1)} %bitcast.10), calls=%async_computation.2 | async-start | bytes 1310720 | tf_op jit(solution)/shard_map/all_to_all | solution.py:72
  53.0 159.2 %reduce-scatter.4.cloned.1.call-start = ((), (), s32[]{:S(2)}) async-start(), calls=%async_computation.9 | async-start | bytes 4177920 | tf_op jit(solution)/shard_map/reduce_scatter | solution.py:83
  63.0 216.3 %all-gather.4.cloned.1.call-start = ((), (), s32[]{:S(2)}) async-start(), calls=%async_computation.6 | async-start | bytes 2088960 | tf_op jit(solution)/shard_map/all_gather | solution.py:94
  66.1 118.1 %copy-start.3 = (bf16[32,40,256]{2,1,0:T(8,128)(2,1)}, bf16[32,40,256]{2,1,0:T(8,128)(2,1)S(1)}, u32[]{:S(2)}) copy-start(bf16[32,40,256]{2,1,0:T(8,128)(2,1)S(1)} %all-to-all-done.2) | copy-start | bytes 1966084
  214.1 138.3 %all-gather.6.cloned.1.call-start = ((), (), s32[]{:S(2)}) async-start(), calls=%async_computation.7 | async-start | bytes 2088960 | tf_op jit(solution)/shard_map/all_gather | solution.py:116
  214.8 209.8 %all-gather.8.cloned.1.call-start = ((), (), s32[]{:S(2)}) async-start(), calls=%async_computation.8 | async-start | bytes 2088960 | tf_op jit(solution)/shard_map/all_gather | solution.py:117
  282.4 158.8 %all-to-all-start.1 = ((bf16[32,40,256]{2,1,0:T(8,128)(2,1)}), bf16[32,40,256]{2,1,0:T(8,128)(2,1)S(1)}, u32[]{:S(2)}, u32[]{:S(2)}) async-start(bf16[32,40,256]{2,1,0:T(8,128)(2,1)} %bitcast.7), calls=%async_computation.1 | async-start | bytes 1310720 | tf_op jit(solution)/shard_map/all_to_all | solution.py:98
  355.4 82.8 %collective-permute-start = (bf16[256,768]{1,0:T(8,128)(2,1)}, bf16[256,768]{1,0:T(8,128)(2,1)}, u32[]{:S(2)}, u32[]{:S(2)}) collective-permute-start(bf16[256,768]{1,0:T(8,128)(2,1)} %get-tuple-element.8), channel_id=1, source_target_pairs={{0,16},{1,17},{2,18},{3,19},{4,20},{5,21},{6,22},{7,23},{8,24},{9,... | collective-permute-start | bytes 1179656 | tf_op jit(solution)/shard_map/ppermute | solution.py:10
  424.7 7.2 %copy-start.4 = (bf16[32,40,256]{2,1,0:T(8,128)(2,1)S(1)}, bf16[32,40,256]{2,1,0:T(8,128)(2,1)}, u32[]{:S(2)}) copy-start(bf16[32,40,256]{2,1,0:T(8,128)(2,1)} %copy-done.3) | copy-start | bytes 1966084
  424.7 7.2 %copy-start.13 = (bf16[1280,768]{1,0:T(8,128)(2,1)S(1)}, bf16[1280,768]{1,0:T(8,128)(2,1)}, u32[]{:S(2)}) copy-start(bf16[1280,768]{1,0:T(8,128)(2,1)} %all-gather.4.cloned.1.call-done) | copy-start | bytes 5898244
  427.1 8.8 %copy-start.1 = (bf16[1280,768]{1,0:T(8,128)(2,1)S(1)}, bf16[1280,768]{1,0:T(8,128)(2,1)}, u32[]{:S(2)}) copy-start(bf16[1280,768]{1,0:T(8,128)(2,1)} %all-gather.6.cloned.1.call-done) | copy-start | bytes 5898244
  427.1 13.1 %collective-permute-start.1 = (bf16[256,768]{1,0:T(8,128)(2,1)S(1)}, bf16[256,768]{1,0:T(8,128)(2,1)S(1)}, u32[]{:S(2)}, u32[]{:S(2)}) collective-permute-start(bf16[256,768]{1,0:T(8,128)(2,1)S(1)} %get-tuple-element.10), channel_id=1, source_target_pairs={{0,16},{1,17},{2,18},{3,19},{4,20},{5,21},{6,22},{7,23},{8,24},{9,... | collective-permute-start | bytes 1179656 | tf_op jit(solution)/shard_map/ppermute | solution.py:10
  433.6 3.0 copy-start.2
  433.6 3.0 copy-start.7
  433.6 25.5 %collective-permute-start.2 = (bf16[768,256]{1,0:T(8,128)(2,1)}, bf16[768,256]{1,0:T(8,128)(2,1)}, u32[]{:S(2)}, u32[]{:S(2)}) collective-permute-start(bf16[768,256]{1,0:T(8,128)(2,1)} %get-tuple-element.12), channel_id=1, source_target_pairs={{0,16},{1,17},{2,18},{3,19},{4,20},{5,21},{6,22},{7,23},{8,24},{9,... | collective-permute-start | bytes 1179656 | tf_op jit(solution)/shard_map/ppermute | solution.py:10
  440.2 19.0 %copy-start.8 = (f32[768,256]{1,0:T(8,128)S(1)}, f32[768,256]{1,0:T(8,128)}, u32[]{:S(2)}) copy-start(f32[768,256]{1,0:T(8,128)} %get-tuple-element.13) | copy-start | bytes 2359300
  441.1 30.9 %all-to-all-start.4 = ((bf16[32,40,256]{2,1,0:T(8,128)(2,1)}), bf16[32,40,256]{2,1,0:T(8,128)(2,1)}, u32[]{:S(2)}, u32[]{:S(2)}) async-start(bf16[32,40,256]{2,1,0:T(8,128)(2,1)} %bitcast.13), calls=%async_computation.4 | async-start | bytes 1310720 | tf_op jit(solution)/shard_map/all_to_all | solution.py:125
  461.1 11.0 %copy-start.10 = (pred[1280,128]{1,0:T(8,128)(4,1)S(1)}, pred[1280,128]{1,0:T(8,128)(4,1)}, u32[]{:S(2)}) copy-start(pred[1280,128]{1,0:T(8,128)(4,1)} %copy-done.9) | copy-start | bytes 491524
Sparse Core Ops, SparseCore 0:
  63.1 149.0 reduce-scatter.3
  214.5 64.7 all-gather.3
  282.1 70.2 all-gather.5
  355.2 69.4 all-gather.7
where the time goes:
time: 482 us; the launch traced here: 481 us
  waiting for transfers between devices  226 us (47%)
  blocking collectives  117 us (24%)
  starting transfers between devices  62 us (13%)
  other arithmetic  30.5 us (6%)
  matrix products  22 us (5%)
  between operations  14.7 us (3%)
  local copies, waits for them, and re-layouts  7.99 us (2%)
    all_to_all x1, blocking collectives, per_device(): lax.all_to_all(hidden_parts, 'dp', split_axis=0, concat_axis=0, tiled=True)  117 us
    all_gather x1, waiting for transfers between devices, per_device(): piece_up = lax.all_gather(grad_up_rows, 'dp', axis=0, tiled=True)  64.6 us
    all_gather x1, waiting for transfers between devices, per_device(): piece = lax.all_gather(hid_own, 'dp', axis=0, tiled=True)  56.5 us
    all_gather x1, waiting for transfers between devices, per_device(): piece_gate = lax.all_gather(grad_gate_rows, 'dp', axis=0, tiled=True)  52.7 us
    reduce_scatter x1, waiting for transfers between devices, per_device(): lax.psum_scatter(rounded(jnp.concatenate([product(block_rows, gate_slab),...  27.7 us
    all_to_all x1, starting transfers between devices, per_device(): lax.all_to_all(back_slab.reshape(n_expert, capacity, slab), 'expert', spl...  18 us
    all_to_all x1, starting transfers between devices, per_device(): lax.all_to_all(answer_slab.reshape(n_expert, capacity, slab), 'expert', s...  17.4 us
    ppermute x3, starting transfers between devices, swapped(): return lax.ppermute(value, axis, pairs)  11.7 us
  transfers between devices with their start and end apart: 11, of which 7 were waited for; matrix products, arithmetic and copies ran while one was open for 8% of the time, Pallas kernels for 0%

commit v1 on v0

--- a/solution.py
+++ b/solution.py
@@ -2,6 +2,17 @@
 import jax.numpy as jnp
 from jax import lax
 from jax.sharding import PartitionSpec as P
+
+
+def around_the_ring(shard, axis, dim):
+    devices = lax.axis_size(axis)
+    route = [(i, (i + 1) % devices) for i in range(devices)]
+    parts = [shard]
+    for far in range(1, devices):
+        parts = [lax.ppermute(parts[0], axis, route), *parts]
+    whole = jnp.concatenate(parts, axis=dim)
+    shift = (lax.axis_index(axis) + 1) * parts[-1].shape[dim]
+    return jnp.roll(whole, shift, axis=dim)
 
 
 def swapped(value, axis, stride):
@@ -114,7 +125,7 @@
     )
     grad_up_rows = (grad_hidden * activated).astype(jnp.bfloat16)
     piece_gate = lax.all_gather(grad_gate_rows, "dp", axis=0, tiled=True)
-    piece_up = lax.all_gather(grad_up_rows, "dp", axis=0, tiled=True)
+    piece_up = around_the_ring(grad_up_rows, "dp", 0)
     block_rows = token_slab
     gate_acc = inner_rows(block_rows, piece_gate)
     up_acc = inner_rows(block_rows, piece_up)

time: 482 us -> 451 us (0.936)
  waiting for transfers between devices: 226 us -> 154 us
  starting transfers between devices: 62 us -> 99.8 us
    ppermute x0 -> x15, waiting for transfers between devices: none -> 81.8 us  [around_the_ring(): parts = [lax.ppermute(parts[0], axis, route), *parts]]
    all_gather x1 -> x0, waiting for transfers between devices: 64.6 us -> none  [per_device(): piece_up = lax.all_gather(grad_up_rows, 'dp', axis=0, tiled=True)]
    all_gather x1, waiting for transfers between devices: 52.7 us -> 0.01 us  [per_device(): piece_gate = lax.all_gather(grad_gate_rows, 'dp', axis=0, tiled=True)]
    all_gather x1, waiting for transfers between devices: 56.5 us -> 23.6 us  [per_device(): piece = lax.all_gather(hid_own, 'dp', axis=0, tiled=True)]
    ppermute x0 -> x15, starting transfers between devices: none -> 31 us  [around_the_ring(): parts = [lax.ppermute(parts[0], axis, route), *parts]]
    all_to_all x1, waiting for transfers between devices: 9.76 us -> 0.01 us  [per_device(): lax.all_to_all(back_slab.reshape(n_expert, capacity, slab), 'expert', spl...]
    all_to_all x1, waiting for transfers between devices: 0.01 us -> 6.86 us  [per_device(): lax.all_to_all(answer_slab.reshape(n_expert, capacity, slab), 'expert', s...]
    all_to_all x1, starting transfers between devices: 18 us -> 24.2 us  [per_device(): lax.all_to_all(back_slab.reshape(n_expert, capacity, slab), 'expert', spl...]
  transfers between devices with their start and end apart: 11 -> 25, of which waited for: 7 -> 20; matrix products, arithmetic and copies ran while one was open for 8% -> 9% of each run, Pallas kernels for 0% -> 0%
where the time goes in v1:
time: 451 us; the launch traced here: 450 us
  waiting for transfers between devices  154 us (34%)
  blocking collectives  117 us (26%)
  starting transfers between devices  99.8 us (22%)
  other arithmetic  31.3 us (7%)
  matrix products  22.4 us (5%)
  between operations  15.1 us (3%)
  local copies, waits for them, and re-layouts  10.2 us (2%)
    all_to_all x1, blocking collectives, per_device(): lax.all_to_all(hidden_parts, 'dp', split_axis=0, concat_axis=0, tiled=True)  117 us
    ppermute x15, waiting for transfers between devices, around_the_ring(): parts = [lax.ppermute(parts[0], axis, route), *parts]  81.8 us
    ppermute x15, starting transfers between devices, around_the_ring(): parts = [lax.ppermute(parts[0], axis, route), *parts]  31 us
    reduce_scatter x1, waiting for transfers between devices, per_device(): lax.psum_scatter(rounded(jnp.concatenate([product(block_rows, gate_slab),...  27.7 us
    all_to_all x1, starting transfers between devices, per_device(): lax.all_to_all(back_slab.reshape(n_expert, capacity, slab), 'expert', spl...  24.2 us
    all_gather x1, waiting for transfers between devices, per_device(): piece = lax.all_gather(hid_own, 'dp', axis=0, tiled=True)  23.6 us
    ppermute x3, starting transfers between devices, swapped(): return lax.ppermute(value, axis, pairs)  15 us
    all_to_all x1, starting transfers between devices, per_device(): lax.all_to_all(answer_slab.reshape(n_expert, capacity, slab), 'expert', s...  14.9 us
  transfers between devices with their start and end apart: 25, of which 20 were waited for; matrix products, arithmetic and copies ran while one was open for 9% of the time, Pallas kernels for 0%

profile of v1, /device:TPU:1, one launch (start us, length us, event | category | flops | bytes accessed | tf_op | source)
XLA Modules:
  0.0 450.0 jit_solution(10655276451003950678)
XLA Ops:
  8.2 9.0 %reduce-window.6 = s32[32,8,128]{2,1,0:T(8,128)S(1)} reduce-window(s32[32,8,128]{2,1,0:T(8,128)S(1)} %fusion.27, s32[]{:T(128)} %constant.35.clone.1), window={size=1x1x128 pad=0_0x0_0x127_0}, to_apply=%region_0.0 | reduce-window | flops 4161536 | bytes 262148 | tf_op jit(solution)/shard_map/reduce-window
  18.6 4.6 %fusion = pred[1280,128]{1,0:T(8,128)(4,1)S(1)} fusion(s32[128,8]{0,1:T(8,128)S(1)} %multiply_add_fusion.1), kind=kLoop, calls=%fused_computation.3 | loop fusion | flops 2457600 | bytes 167936 | tf_op jit(solution)/shard_map/reduce_or | solution.py:64
  25.4 10.4 %all-to-all-start = ((bf16[32,40,256]{2,1,0:T(8,128)(2,1)}), bf16[32,40,256]{2,1,0:T(8,128)(2,1)S(1)}, u32[]{:S(2)}, u32[]{:S(2)}) async-start(bf16[32,40,256]{2,1,0:T(8,128)(2,1)} %bitcast.2), calls=%async_computation | async-start | bytes 1310720 | tf_op jit(solution)/shard_map/all_to_all | solution.py:76
  38.0 10.8 %all-to-all-done = bf16[32,40,256]{2,1,0:T(8,128)(2,1)S(1)} async-done(((bf16[32,40,256]{2,1,0:T(8,128)(2,1)}), bf16[32,40,256]{2,1,0:T(8,128)(2,1)S(1)}, u32[]{:S(2)}, u32[]{:S(2)}) %all-to-all-start) | async-done | bytes 655392 | tf_op jit(solution)/shard_map/all_to_all | solution.py:76
  48.8 4.1 all-to-all-start.2
  56.6 6.3 %copy.48 = bf16[1280,1536]{1,0:T(8,128)(2,1)} copy(bf16[1280,1536]{0,1:T(8,128)(2,1)} %pad_maximum_fusion) | data formatting | bytes 7864320
  66.7 117.4 %all_to_all.25 = bf16[16,80,768]{2,1,0:T(8,128)(2,1)S(1)} all-to-all(bf16[16,80,768]{2,1,0:T(8,128)(2,1)S(1)} %bitcast.75), channel_id=1, replica_groups=mesh['dp'=16,'expert'=32] {'dp'}, dimensions={0} | all-to-all | bytes 3932160 | tf_op jit(solution)/shard_map/all_to_all | solution.py:119
  184.3 27.7 %reduce-scatter.4.cloned.1.call-done = bf16[80,1536]{1,0:T(8,128)(2,1)} async-done(((bf16[1280,1536]{1,0:T(8,128)(2,1)}), bf16[80,1536]{1,0:T(8,128)(2,1)}) %reduce-scatter.4.cloned.1.call-update) | async-done | bytes 245776 | tf_op jit(solution)/shard_map/reduce_scatter | solution.py:94
  213.9 3.6 collective-permute-start
  223.1 4.7 %collective-permute-done.1 = bf16[80,768]{1,0:T(8,128)(2,1)S(1)} collective-permute-done((bf16[80,768]{1,0:T(8,128)(2,1)S(1)}, bf16[80,768]{1,0:T(8,128)(2,1)S(1)}, u32[]{:S(2)}, u32[]{:S(2)}) %collective-permute-start.1) | collective-permute-done | bytes 122912 | tf_op jit(solution)/shard_map/ppermute | solution.py:12
  229.8 6.4 %collective-permute-done.2 = bf16[80,768]{1,0:T(8,128)(2,1)S(1)} collective-permute-done((bf16[80,768]{1,0:T(8,128)(2,1)S(1)}, bf16[80,768]{1,0:T(8,128)(2,1)S(1)}, u32[]{:S(2)}, u32[]{:S(2)}) %collective-permute-start.2) | collective-permute-done | bytes 122912 | tf_op jit(solution)/shard_map/ppermute | solution.py:12
  238.1 7.9 %collective-permute-done.3 = bf16[80,768]{1,0:T(8,128)(2,1)S(1)} collective-permute-done((bf16[80,768]{1,0:T(8,128)(2,1)S(1)}, bf16[80,768]{1,0:T(8,128)(2,1)S(1)}, u32[]{:S(2)}, u32[]{:S(2)}) %collective-permute-start.3) | collective-permute-done | bytes 122912 | tf_op jit(solution)/shard_map/ppermute | solution.py:12
  247.9 5.6 %collective-permute-done.4 = bf16[80,768]{1,0:T(8,128)(2,1)S(1)} collective-permute-done((bf16[80,768]{1,0:T(8,128)(2,1)S(1)}, bf16[80,768]{1,0:T(8,128)(2,1)S(1)}, u32[]{:S(2)}, u32[]{:S(2)}) %collective-permute-start.4) | collective-permute-done | bytes 122912 | tf_op jit(solution)/shard_map/ppermute | solution.py:12
  255.5 5.1 %collective-permute-done.5 = bf16[80,768]{1,0:T(8,128)(2,1)S(1)} collective-permute-done((bf16[80,768]{1,0:T(8,128)(2,1)S(1)}, bf16[80,768]{1,0:T(8,128)(2,1)S(1)}, u32[]{:S(2)}, u32[]{:S(2)}) %collective-permute-start.5) | collective-permute-done | bytes 122912 | tf_op jit(solution)/shard_map/ppermute | solution.py:12
  262.6 5.9 %collective-permute-done.6 = bf16[80,768]{1,0:T(8,128)(2,1)S(1)} collective-permute-done((bf16[80,768]{1,0:T(8,128)(2,1)S(1)}, bf16[80,768]{1,0:T(8,128)(2,1)S(1)}, u32[]{:S(2)}, u32[]{:S(2)}) %collective-permute-start.6) | collective-permute-done | bytes 122912 | tf_op jit(solution)/shard_map/ppermute | solution.py:12
  270.4 5.7 %collective-permute-done.7 = bf16[80,768]{1,0:T(8,128)(2,1)S(1)} collective-permute-done((bf16[80,768]{1,0:T(8,128)(2,1)S(1)}, bf16[80,768]{1,0:T(8,128)(2,1)S(1)}, u32[]{:S(2)}, u32[]{:S(2)}) %collective-permute-start.7) | collective-permute-done | bytes 122912 | tf_op jit(solution)/shard_map/ppermute | solution.py:12
  277.9 5.7 %collective-permute-done.8 = bf16[80,768]{1,0:T(8,128)(2,1)S(1)} collective-permute-done((bf16[80,768]{1,0:T(8,128)(2,1)S(1)}, bf16[80,768]{1,0:T(8,128)(2,1)S(1)}, u32[]{:S(2)}, u32[]{:S(2)}) %collective-permute-start.8) | collective-permute-done | bytes 122912 | tf_op jit(solution)/shard_map/ppermute | solution.py:12
  285.6 6.2 %collective-permute-done.9 = bf16[80,768]{1,0:T(8,128)(2,1)S(1)} collective-permute-done((bf16[80,768]{1,0:T(8,128)(2,1)S(1)}, bf16[80,768]{1,0:T(8,128)(2,1)S(1)}, u32[]{:S(2)}, u32[]{:S(2)}) %collective-permute-start.9) | collective-permute-done | bytes 122912 | tf_op jit(solution)/shard_map/ppermute | solution.py:12
  293.7 5.9 %collective-permute-done.10 = bf16[80,768]{1,0:T(8,128)(2,1)S(1)} collective-permute-done((bf16[80,768]{1,0:T(8,128)(2,1)S(1)}, bf16[80,768]{1,0:T(8,128)(2,1)S(1)}, u32[]{:S(2)}, u32[]{:S(2)}) %collective-permute-start.10) | collective-permute-done | bytes 122912 | tf_op jit(solution)/shard_map/ppermute | solution.py:12
  301.4 4.9 %collective-permute-done.11 = bf16[80,768]{1,0:T(8,128)(2,1)S(1)} collective-permute-done((bf16[80,768]{1,0:T(8,128)(2,1)S(1)}, bf16[80,768]{1,0:T(8,128)(2,1)S(1)}, u32[]{:S(2)}, u32[]{:S(2)}) %collective-permute-start.11) | collective-permute-done | bytes 122912 | tf_op jit(solution)/shard_map/ppermute | solution.py:12
  308.3 4.9 %collective-permute-done.12 = bf16[80,768]{1,0:T(8,128)(2,1)S(1)} collective-permute-done((bf16[80,768]{1,0:T(8,128)(2,1)S(1)}, bf16[80,768]{1,0:T(8,128)(2,1)S(1)}, u32[]{:S(2)}, u32[]{:S(2)}) %collective-permute-start.12) | collective-permute-done | bytes 122912 | tf_op jit(solution)/shard_map/ppermute | solution.py:12
  315.1 4.9 %collective-permute-done.13 = bf16[80,768]{1,0:T(8,128)(2,1)S(1)} collective-permute-done((bf16[80,768]{1,0:T(8,128)(2,1)S(1)}, bf16[80,768]{1,0:T(8,128)(2,1)S(1)}, u32[]{:S(2)}, u32[]{:S(2)}) %collective-permute-start.13) | collective-permute-done | bytes 122912 | tf_op jit(solution)/shard_map/ppermute | solution.py:12
  322.0 4.9 %collective-permute-done.14 = bf16[80,768]{1,0:T(8,128)(2,1)S(1)} collective-permute-done((bf16[80,768]{1,0:T(8,128)(2,1)S(1)}, bf16[80,768]{1,0:T(8,128)(2,1)S(1)}, u32[]{:S(2)}, u32[]{:S(2)}) %collective-permute-start.14) | collective-permute-done | bytes 122912 | tf_op jit(solution)/shard_map/ppermute | solution.py:12
  330.1 5.4 %collective-permute-start.16 = (bf16[256,768]{1,0:T(8,128)(2,1)S(1)}, bf16[256,768]{1,0:T(8,128)(2,1)S(1)}, u32[]{:S(2)}, u32[]{:S(2)}) collective-permute-start(bf16[256,768]{1,0:T(8,128)(2,1)S(1)} %get-tuple-element.10), channel_id=1, source_target_pairs={{0,16},{1,17},{2,18},{3,19},{4,20},{5,21},{6,22},{7,23},{8,24},{9,... | collective-permute-start | bytes 1179656 | tf_op jit(solution)/shard_map/ppermute | solution.py:21
  336.1 7.6 %select_reduce_fusion = f32[1280,128]{1,0:T(8,128)} fusion(f32[128,8]{0,1:T(8,128)S(1)} %copy-done.12, s32[128,8]{0,1:T(8,128)S(1)} %multiply_add_fusion.1), kind=kLoop, calls=%fused_computation.1 | loop fusion | flops 3768320 | bytes 663552 | tf_op jit(solution)/shard_map/reduce_sum | solution.py:65
  350.3 24.2 %all-to-all-start.4 = ((bf16[32,40,256]{2,1,0:T(8,128)(2,1)}), bf16[32,40,256]{2,1,0:T(8,128)(2,1)}, u32[]{:S(2)}, u32[]{:S(2)}) async-start(bf16[32,40,256]{2,1,0:T(8,128)(2,1)} %bitcast.78), calls=%async_computation.4 | async-start | bytes 1310720 | tf_op jit(solution)/shard_map/all_to_all | solution.py:136
  376.3 4.9 %collective-permute-start.15 = (bf16[256,768]{1,0:T(8,128)(2,1)}, bf16[256,768]{1,0:T(8,128)(2,1)}, u32[]{:S(2)}, u32[]{:S(2)}) collective-permute-start(bf16[256,768]{1,0:T(8,128)(2,1)} %get-tuple-element.8), channel_id=1, source_target_pairs={{0,16},{1,17},{2,18},{3,19},{4,20},{5,21},{6,22},{7,23},{8,24},{9,... | collective-permute-start | bytes 1179656 | tf_op jit(solution)/shard_map/ppermute | solution.py:21
  381.2 23.6 %all-gather.3.cloned.1.call-done = bf16[1280,768]{1,0:T(8,128)(2,1)} async-done(((bf16[80,768]{1,0:T(8,128)(2,1)}), bf16[1280,768]{1,0:T(8,128)(2,1)}) %all-gather.3.cloned.1.call-update) | async-done | bytes 1966096 | tf_op jit(solution)/shard_map/all_gather | solution.py:105
  404.8 3.3 fusion.32
  408.1 4.7 %collective-permute-start.17 = (bf16[768,256]{1,0:T(8,128)(2,1)}, bf16[768,256]{1,0:T(8,128)(2,1)}, u32[]{:S(2)}, u32[]{:S(2)}) collective-permute-start(bf16[768,256]{1,0:T(8,128)(2,1)} %get-tuple-element.12), channel_id=1, source_target_pairs={{0,16},{1,17},{2,18},{3,19},{4,20},{5,21},{6,22},{7,23},{8,24},{9,... | collective-permute-start | bytes 1179656 | tf_op jit(solution)/shard_map/ppermute | solution.py:21
  414.4 14.9 %all-to-all-start.1 = ((bf16[32,40,256]{2,1,0:T(8,128)(2,1)}), bf16[32,40,256]{2,1,0:T(8,128)(2,1)S(1)}, u32[]{:S(2)}, u32[]{:S(2)}) async-start(bf16[32,40,256]{2,1,0:T(8,128)(2,1)} %bitcast.81), calls=%async_computation.1 | async-start | bytes 1310720 | tf_op jit(solution)/shard_map/all_to_all | solution.py:109
  435.3 6.9 %all-to-all-done.1 = bf16[32,40,256]{2,1,0:T(8,128)(2,1)S(1)} async-done(((bf16[32,40,256]{2,1,0:T(8,128)(2,1)}), bf16[32,40,256]{2,1,0:T(8,128)(2,1)S(1)}, u32[]{:S(2)}, u32[]{:S(2)}) %all-to-all-start.1) | async-done | bytes 655392 | tf_op jit(solution)/shard_map/all_to_all | solution.py:109
  (125 shorter events, 66.7 us)
Async XLA Ops:
  7.2 46.5 %copy-start = (bf16[1,256,768]{2,1,0:T(8,128)(2,1)S(1)}, bf16[1,256,768]{2,1,0:T(8,128)(2,1)}, u32[]{:S(2)}) copy-start(bf16[1,256,768]{2,1,0:T(8,128)(2,1)} %param.12) | copy-start | bytes 1179652
  23.3 29.7 %copy-start.6 = (bf16[1,256,768]{2,1,0:T(8,128)(2,1)S(1)}, bf16[1,256,768]{2,1,0:T(8,128)(2,1)}, u32[]{:S(2)}) copy-start(bf16[1,256,768]{2,1,0:T(8,128)(2,1)} %param.13) | copy-start | bytes 1179652
  25.4 23.5 %all-to-all-start = ((bf16[32,40,256]{2,1,0:T(8,128)(2,1)}), bf16[32,40,256]{2,1,0:T(8,128)(2,1)S(1)}, u32[]{:S(2)}, u32[]{:S(2)}) async-start(bf16[32,40,256]{2,1,0:T(8,128)(2,1)} %bitcast.2), calls=%async_computation | async-start | bytes 1310720 | tf_op jit(solution)/shard_map/all_to_all | solution.py:76
  48.8 17.1 %all-to-all-start.2 = ((bf16[32,40,256]{2,1,0:T(8,128)(2,1)}), bf16[32,40,256]{2,1,0:T(8,128)(2,1)S(1)}, u32[]{:S(2)}, u32[]{:S(2)}) async-start(bf16[32,40,256]{2,1,0:T(8,128)(2,1)} %bitcast.10), calls=%async_computation.2 | async-start | bytes 1310720 | tf_op jit(solution)/shard_map/all_to_all | solution.py:83
  52.9 159.1 %reduce-scatter.4.cloned.1.call-start = ((), (), s32[]{:S(2)}) async-start(), calls=%async_computation.8 | async-start | bytes 4177920 | tf_op jit(solution)/shard_map/reduce_scatter | solution.py:94
  62.9 281.8 %all-gather.5.cloned.1.call-start = ((), (), s32[]{:S(2)}) async-start(), calls=%async_computation.7 | async-start | bytes 2088960 | tf_op jit(solution)/shard_map/all_gather | solution.py:127
  65.9 118.4 %copy-start.5 = (bf16[32,40,256]{2,1,0:T(8,128)(2,1)}, bf16[32,40,256]{2,1,0:T(8,128)(2,1)S(1)}, u32[]{:S(2)}) copy-start(bf16[32,40,256]{2,1,0:T(8,128)(2,1)S(1)} %all-to-all-done.2) | copy-start | bytes 1966084
  213.8 191.0 %all-gather.3.cloned.1.call-start = ((), (), s32[]{:S(2)}) async-start(), calls=%async_computation.6 | async-start | bytes 2088960 | tf_op jit(solution)/shard_map/all_gather | solution.py:105
  213.9 6.8 %collective-permute-start = (bf16[80,768]{1,0:T(8,128)(2,1)S(1)}, bf16[80,768]{1,0:T(8,128)(2,1)S(1)}, u32[]{:S(2)}, u32[]{:S(2)}) collective-permute-start(bf16[80,768]{1,0:T(8,128)(2,1)S(1)} %get-tuple-element.5), channel_id=1, source_target_pairs={{0,32},{32,64},{64,96},{96,128},{128,160},{160,192},{192,224},{224... | collective-permute-start | bytes 368648 | tf_op jit(solution)/shard_map/ppermute | solution.py:12
  220.7 7.1 %collective-permute-start.1 = (bf16[80,768]{1,0:T(8,128)(2,1)S(1)}, bf16[80,768]{1,0:T(8,128)(2,1)S(1)}, u32[]{:S(2)}, u32[]{:S(2)}) collective-permute-start(bf16[80,768]{1,0:T(8,128)(2,1)S(1)} %collective-permute-done), channel_id=1, source_target_pairs={{0,32},{32,64},{64,96},{96,128},{128,160},{160,192},{192,224},{224... | collective-permute-start | bytes 368648 | tf_op jit(solution)/shard_map/ppermute | solution.py:12
  227.8 8.3 %collective-permute-start.2 = (bf16[80,768]{1,0:T(8,128)(2,1)S(1)}, bf16[80,768]{1,0:T(8,128)(2,1)S(1)}, u32[]{:S(2)}, u32[]{:S(2)}) collective-permute-start(bf16[80,768]{1,0:T(8,128)(2,1)S(1)} %collective-permute-done.1), channel_id=1, source_target_pairs={{0,32},{32,64},{64,96},{96,128},{128,160},{160,192},{192,224},{224... | collective-permute-start | bytes 368648 | tf_op jit(solution)/shard_map/ppermute | solution.py:12
  236.1 9.8 %collective-permute-start.3 = (bf16[80,768]{1,0:T(8,128)(2,1)S(1)}, bf16[80,768]{1,0:T(8,128)(2,1)S(1)}, u32[]{:S(2)}, u32[]{:S(2)}) collective-permute-start(bf16[80,768]{1,0:T(8,128)(2,1)S(1)} %collective-permute-done.2), channel_id=1, source_target_pairs={{0,32},{32,64},{64,96},{96,128},{128,160},{160,192},{192,224},{224... | collective-permute-start | bytes 368648 | tf_op jit(solution)/shard_map/ppermute | solution.py:12
  246.0 7.6 %collective-permute-start.4 = (bf16[80,768]{1,0:T(8,128)(2,1)S(1)}, bf16[80,768]{1,0:T(8,128)(2,1)S(1)}, u32[]{:S(2)}, u32[]{:S(2)}) collective-permute-start(bf16[80,768]{1,0:T(8,128)(2,1)S(1)} %collective-permute-done.3), channel_id=1, source_target_pairs={{0,32},{32,64},{64,96},{96,128},{128,160},{160,192},{192,224},{224... | collective-permute-start | bytes 368648 | tf_op jit(solution)/shard_map/ppermute | solution.py:12
  253.5 7.2 %collective-permute-start.5 = (bf16[80,768]{1,0:T(8,128)(2,1)S(1)}, bf16[80,768]{1,0:T(8,128)(2,1)S(1)}, u32[]{:S(2)}, u32[]{:S(2)}) collective-permute-start(bf16[80,768]{1,0:T(8,128)(2,1)S(1)} %collective-permute-done.4), channel_id=1, source_target_pairs={{0,32},{32,64},{64,96},{96,128},{128,160},{160,192},{192,224},{224... | collective-permute-start | bytes 368648 | tf_op jit(solution)/shard_map/ppermute | solution.py:12
  260.7 7.8 %collective-permute-start.6 = (bf16[80,768]{1,0:T(8,128)(2,1)S(1)}, bf16[80,768]{1,0:T(8,128)(2,1)S(1)}, u32[]{:S(2)}, u32[]{:S(2)}) collective-permute-start(bf16[80,768]{1,0:T(8,128)(2,1)S(1)} %collective-permute-done.5), channel_id=1, source_target_pairs={{0,32},{32,64},{64,96},{96,128},{128,160},{160,192},{192,224},{224... | collective-permute-start | bytes 368648 | tf_op jit(solution)/shard_map/ppermute | solution.py:12
  268.4 7.6 %collective-permute-start.7 = (bf16[80,768]{1,0:T(8,128)(2,1)S(1)}, bf16[80,768]{1,0:T(8,128)(2,1)S(1)}, u32[]{:S(2)}, u32[]{:S(2)}) collective-permute-start(bf16[80,768]{1,0:T(8,128)(2,1)S(1)} %collective-permute-done.6), channel_id=1, source_target_pairs={{0,32},{32,64},{64,96},{96,128},{128,160},{160,192},{192,224},{224... | collective-permute-start | bytes 368648 | tf_op jit(solution)/shard_map/ppermute | solution.py:12
  276.0 7.6 %collective-permute-start.8 = (bf16[80,768]{1,0:T(8,128)(2,1)S(1)}, bf16[80,768]{1,0:T(8,128)(2,1)S(1)}, u32[]{:S(2)}, u32[]{:S(2)}) collective-permute-start(bf16[80,768]{1,0:T(8,128)(2,1)S(1)} %collective-permute-done.7), channel_id=1, source_target_pairs={{0,32},{32,64},{64,96},{96,128},{128,160},{160,192},{192,224},{224... | collective-permute-start | bytes 368648 | tf_op jit(solution)/shard_map/ppermute | solution.py:12
  283.6 8.1 %collective-permute-start.9 = (bf16[80,768]{1,0:T(8,128)(2,1)S(1)}, bf16[80,768]{1,0:T(8,128)(2,1)S(1)}, u32[]{:S(2)}, u32[]{:S(2)}) collective-permute-start(bf16[80,768]{1,0:T(8,128)(2,1)S(1)} %collective-permute-done.8), channel_id=1, source_target_pairs={{0,32},{32,64},{64,96},{96,128},{128,160},{160,192},{192,224},{224... | collective-permute-start | bytes 368648 | tf_op jit(solution)/shard_map/ppermute | solution.py:12
  291.7 7.8 %collective-permute-start.10 = (bf16[80,768]{1,0:T(8,128)(2,1)S(1)}, bf16[80,768]{1,0:T(8,128)(2,1)S(1)}, u32[]{:S(2)}, u32[]{:S(2)}) collective-permute-start(bf16[80,768]{1,0:T(8,128)(2,1)S(1)} %collective-permute-done.9), channel_id=1, source_target_pairs={{0,32},{32,64},{64,96},{96,128},{128,160},{160,192},{192,224},{224... | collective-permute-start | bytes 368648 | tf_op jit(solution)/shard_map/ppermute | solution.py:12
  299.5 6.8 %collective-permute-start.11 = (bf16[80,768]{1,0:T(8,128)(2,1)S(1)}, bf16[80,768]{1,0:T(8,128)(2,1)S(1)}, u32[]{:S(2)}, u32[]{:S(2)}) collective-permute-start(bf16[80,768]{1,0:T(8,128)(2,1)S(1)} %collective-permute-done.10), channel_id=1, source_target_pairs={{0,32},{32,64},{64,96},{96,128},{128,160},{160,192},{192,224},{224... | collective-permute-start | bytes 368648 | tf_op jit(solution)/shard_map/ppermute | solution.py:12
  306.4 6.8 %collective-permute-start.12 = (bf16[80,768]{1,0:T(8,128)(2,1)S(1)}, bf16[80,768]{1,0:T(8,128)(2,1)S(1)}, u32[]{:S(2)}, u32[]{:S(2)}) collective-permute-start(bf16[80,768]{1,0:T(8,128)(2,1)S(1)} %collective-permute-done.11), channel_id=1, source_target_pairs={{0,32},{32,64},{64,96},{96,128},{128,160},{160,192},{192,224},{224... | collective-permute-start | bytes 368648 | tf_op jit(solution)/shard_map/ppermute | solution.py:12
  313.2 6.8 %collective-permute-start.13 = (bf16[80,768]{1,0:T(8,128)(2,1)S(1)}, bf16[80,768]{1,0:T(8,128)(2,1)S(1)}, u32[]{:S(2)}, u32[]{:S(2)}) collective-permute-start(bf16[80,768]{1,0:T(8,128)(2,1)S(1)} %collective-permute-done.12), channel_id=1, source_target_pairs={{0,32},{32,64},{64,96},{96,128},{128,160},{160,192},{192,224},{224... | collective-permute-start | bytes 368648 | tf_op jit(solution)/shard_map/ppermute | solution.py:12
  320.0 6.8 %collective-permute-start.14 = (bf16[80,768]{1,0:T(8,128)(2,1)S(1)}, bf16[80,768]{1,0:T(8,128)(2,1)S(1)}, u32[]{:S(2)}, u32[]{:S(2)}) collective-permute-start(bf16[80,768]{1,0:T(8,128)(2,1)S(1)} %collective-permute-done.13), channel_id=1, source_target_pairs={{0,32},{32,64},{64,96},{96,128},{128,160},{160,192},{192,224},{224... | collective-permute-start | bytes 368648 | tf_op jit(solution)/shard_map/ppermute | solution.py:12
  330.1 13.7 %collective-permute-start.16 = (bf16[256,768]{1,0:T(8,128)(2,1)S(1)}, bf16[256,768]{1,0:T(8,128)(2,1)S(1)}, u32[]{:S(2)}, u32[]{:S(2)}) collective-permute-start(bf16[256,768]{1,0:T(8,128)(2,1)S(1)} %get-tuple-element.10), channel_id=1, source_target_pairs={{0,16},{1,17},{2,18},{3,19},{4,20},{5,21},{6,22},{7,23},{8,24},{9,... | collective-permute-start | bytes 1179656 | tf_op jit(solution)/shard_map/ppermute | solution.py:21
  344.7 29.8 %copy-start.1 = (bf16[1280,768]{1,0:T(8,128)(2,1)S(1)}, bf16[1280,768]{1,0:T(8,128)(2,1)}, u32[]{:S(2)}) copy-start(bf16[1280,768]{1,0:T(8,128)(2,1)} %all-gather.5.cloned.1.call-done) | copy-start | bytes 5898244
  350.3 64.1 %all-to-all-start.4 = ((bf16[32,40,256]{2,1,0:T(8,128)(2,1)}), bf16[32,40,256]{2,1,0:T(8,128)(2,1)}, u32[]{:S(2)}, u32[]{:S(2)}) async-start(bf16[32,40,256]{2,1,0:T(8,128)(2,1)} %bitcast.78), calls=%async_computation.4 | async-start | bytes 1310720 | tf_op jit(solution)/shard_map/all_to_all | solution.py:136
  376.3 36.5 %copy-start.10 = (bf16[1,768,256]{2,1,0:T(8,128)(2,1)S(1)}, bf16[1,768,256]{2,1,0:T(8,128)(2,1)}, u32[]{:S(2)}) copy-start(bf16[1,768,256]{2,1,0:T(8,128)(2,1)} %param.14) | copy-start | bytes 1179652
  376.3 53.0 %copy-start.4 = (f32[256,768]{1,0:T(8,128)S(1)}, f32[256,768]{1,0:T(8,128)}, u32[]{:S(2)}) copy-start(f32[256,768]{1,0:T(8,128)} %get-tuple-element.9) | copy-start | bytes 2359300
  376.3 53.0 %collective-permute-start.15 = (bf16[256,768]{1,0:T(8,128)(2,1)}, bf16[256,768]{1,0:T(8,128)(2,1)}, u32[]{:S(2)}, u32[]{:S(2)}) collective-permute-start(bf16[256,768]{1,0:T(8,128)(2,1)} %get-tuple-element.8), channel_id=1, source_target_pairs={{0,16},{1,17},{2,18},{3,19},{4,20},{5,21},{6,22},{7,23},{8,24},{9,... | collective-permute-start | bytes 1179656 | tf_op jit(solution)/shard_map/ppermute | solution.py:21
  408.1 34.1 %copy-start.2 = (f32[1280,128]{1,0:T(8,128)S(1)}, f32[1280,128]{1,0:T(8,128)}, u32[]{:S(2)}) copy-start(f32[1280,128]{1,0:T(8,128)} %select_reduce_fusion) | copy-start | bytes 1966084
  408.1 23.2 %collective-permute-start.17 = (bf16[768,256]{1,0:T(8,128)(2,1)}, bf16[768,256]{1,0:T(8,128)(2,1)}, u32[]{:S(2)}, u32[]{:S(2)}) collective-permute-start(bf16[768,256]{1,0:T(8,128)(2,1)} %get-tuple-element.12), channel_id=1, source_target_pairs={{0,16},{1,17},{2,18},{3,19},{4,20},{5,21},{6,22},{7,23},{8,24},{9,... | collective-permute-start | bytes 1179656 | tf_op jit(solution)/shard_map/ppermute | solution.py:21
  414.4 27.8 %all-to-all-start.1 = ((bf16[32,40,256]{2,1,0:T(8,128)(2,1)}), bf16[32,40,256]{2,1,0:T(8,128)(2,1)S(1)}, u32[]{:S(2)}, u32[]{:S(2)}) async-start(bf16[32,40,256]{2,1,0:T(8,128)(2,1)} %bitcast.81), calls=%async_computation.1 | async-start | bytes 1310720 | tf_op jit(solution)/shard_map/all_to_all | solution.py:109
  (7 other events, 97.4 us)
Sparse Core Ops, SparseCore 0:
  63.0 148.9 reduce-scatter.3
  214.9 68.4 all-gather.4
  322.1 82.6 all-gather.2
